TPU v7x, 256 devices: a whole 4x4x8 slice. The times are simulated.
256 devices in a mesh: seq: 32 (over y, x, core), rep: 8 (over z).
Axes of the slice: x: 4, y: 4, z: 8, core: 2. Of those that a mesh axis runs over, the one named last changes fastest.
Arguments:
- tokens: bfloat16 [8, 4096, 1024], P('rep', 'seq'), may hold values from -16 to 16
- cotangent: bfloat16 [8, 4096, 1024], P('rep', 'seq'), may hold values from -6 to 6
- weights: bfloat16 [4, 1024, 512], replicated, may hold values from -0.1875 to 0.1875
- neighbour_lists: int32 [8, 32, 27], P('rep'), may hold values from 0 to 31, as said below
- neighbour_counts: int32 [8, 32], P('rep'), may hold values from 1 to 27, as said below
Outputs:
- output: bfloat16 [8, 4096, 1024], P('rep', 'seq')
- d_inputs: bfloat16 [8, 4096, 1024], P('rep', 'seq')
- weight_grads: float32 [4, 1024, 512], P(None, ('seq', 'rep'))
Inputs may be any that keep to these rules, and one draw needn't show every extreme that they name: `neighbour_lists`: slot 0 of every list is the block itself; the live slots of a list name distinct blocks of the same replica's slab; dead slots hold the block's own position. `neighbour_counts`: in each replica some block has min(27, 32) live slots.
All inputs are finite; a program needn't handle non-finite values.
Results may differ from a plain program's by a relative error of at most 0.023.
The roundings to bfloat16 on the way count: a program that leaves them out, or rounds other values in their place, can miss the bound.
Values may be sent and summed in bfloat16 or wider, within the bound.
No kernel may reach another device: no remote copies, remote signals or barrier semaphores. Data moves between devices by JAX's collectives and lax.ppermute only.
A program may use at most 128 MiB of HBM per device.

v0:
```python
import math
import jax
import jax.numpy as jnp
from jax import lax
from jax.sharding import PartitionSpec as P

HEADS = 8
HEAD_DIM = 64
BLOCK = 128
MAXN = 27


def split_heads(matrix):
    return matrix.reshape(matrix.shape[:-1] + (HEADS, HEAD_DIM))


def body(tokens, cotangent, weights, neighbour_lists, neighbour_counts):
    score_scale = 1.0 / math.sqrt(HEAD_DIM)
    inputs = tokens[0]
    upstream = cotangent[0]
    row_count = inputs.shape[0]
    local_blocks = row_count // BLOCK
    w_query, w_key, w_value, w_out = (weights[0], weights[1], weights[2], weights[3])
    queries = (
        jnp.dot(inputs, w_query, preferred_element_type=jnp.float32)
        .astype(jnp.bfloat16)
        .reshape(local_blocks, BLOCK, -1)
    )
    key_rows = (
        jnp.dot(inputs, w_key, preferred_element_type=jnp.float32)
        .astype(jnp.bfloat16)
        .reshape(local_blocks, BLOCK, -1)
    )
    value_rows = (
        jnp.dot(inputs, w_value, preferred_element_type=jnp.float32)
        .astype(jnp.bfloat16)
        .reshape(local_blocks, BLOCK, -1)
    )
    all_keys, all_values = (
        lax.all_gather(key_rows, "seq", axis=0, tiled=True),
        lax.all_gather(value_rows, "seq", axis=0, tiled=True),
    )
    slab_blocks = all_keys.shape[0]
    first_block = lax.axis_index("seq") * local_blocks
    lists_all = neighbour_lists[0]
    counts_all = neighbour_counts[0]
    my_lists = lax.dynamic_slice_in_dim(lists_all, first_block, local_blocks, 0)
    my_counts = lax.dynamic_slice_in_dim(counts_all, first_block, local_blocks, 0)
    slot_keys = split_heads(
        jnp.take(all_keys, my_lists, axis=0).reshape(local_blocks, MAXN * BLOCK, -1)
    )
    slot_values = split_heads(
        jnp.take(all_values, my_lists, axis=0).reshape(local_blocks, MAXN * BLOCK, -1)
    )
    query_heads = split_heads(queries)
    scores = (
        jnp.einsum("bqhd,bkhd->bhqk", query_heads, slot_keys, preferred_element_type=jnp.float32)
        * score_scale
    )
    live_cols = (jnp.arange(MAXN * BLOCK) // BLOCK)[None, :] < my_counts[:, None]
    scores = jnp.where(live_cols[:, None, None, :], scores, -1e30)
    row_max = jnp.max(scores, axis=-1)
    exponent = jnp.exp(scores - row_max[..., None])
    totals = jnp.sum(exponent, axis=-1)
    mixed = jnp.einsum(
        "bhqk,bkhd->bqhd",
        exponent.astype(jnp.bfloat16),
        slot_values,
        preferred_element_type=jnp.float32,
    )
    attended = (
        (mixed / jnp.transpose(totals, (0, 2, 1))[..., None])
        .astype(jnp.bfloat16)
        .reshape(row_count, -1)
    )
    output = lax.dot_general(
        attended, w_out, (((1,), (1,)), ((), ())), preferred_element_type=jnp.float32
    ).astype(jnp.bfloat16)
    d_attended = jnp.dot(upstream, w_out, preferred_element_type=jnp.float32).astype(jnp.bfloat16)
    grad_out = lax.dot_general(
        upstream, attended, (((0,), (0,)), ((), ())), preferred_element_type=jnp.float32
    )
    d_blocks = d_attended.reshape(local_blocks, BLOCK, -1)
    d_heads = split_heads(d_blocks)
    attended_heads = split_heads(attended.reshape(local_blocks, BLOCK, -1))
    row_delta = jnp.transpose(
        jnp.sum(d_heads.astype(jnp.float32) * attended_heads.astype(jnp.float32), axis=-1),
        (0, 2, 1),
    )
    normed = exponent / totals[..., None]
    d_probs = jnp.einsum(
        "bqhd,bkhd->bhqk", d_heads, slot_values, preferred_element_type=jnp.float32
    )
    d_scores = (normed * (d_probs - row_delta[..., None])).astype(jnp.bfloat16)
    d_queries = (
        (
            jnp.einsum("bhqk,bkhd->bqhd", d_scores, slot_keys, preferred_element_type=jnp.float32)
            * score_scale
        )
        .astype(jnp.bfloat16)
        .reshape(row_count, -1)
    )
    gathered_query, gathered_dattn = (
        lax.all_gather(queries, "seq", axis=0, tiled=True),
        lax.all_gather(d_blocks, "seq", axis=0, tiled=True),
    )
    gathered_max, gathered_total, gathered_delta = (
        lax.all_gather(row_max, "seq", axis=0, tiled=True),
        lax.all_gather(totals, "seq", axis=0, tiled=True),
        lax.all_gather(row_delta, "seq", axis=0, tiled=True),
    )
    owners = first_block + jnp.arange(local_blocks)
    live_slots = jnp.arange(MAXN)[None, :] < counts_all[:, None]
    listed = jnp.any(
        (lists_all[:, :, None] == owners[None, None, :]) & live_slots[:, :, None], axis=1
    )
    groups = slab_blocks // 8
    own_keys = split_heads(key_rows)
    own_values = split_heads(value_rows)

    def regroup(matrix):
        return matrix.reshape((groups, 8) + matrix.shape[1:])

    def accumulate(carry, group_data):
        group_query, group_dattn, group_max, group_total, group_delta, group_listed = group_data
        group_query = split_heads(group_query)
        group_dattn = split_heads(group_dattn)
        group_scores = (
            jnp.einsum(
                "cqhd,ikhd->cihqk", group_query, own_keys, preferred_element_type=jnp.float32
            )
            * score_scale
        )
        group_scores = jnp.where(group_listed[:, :, None, None, None], group_scores, -1e30)
        group_probs = (
            jnp.exp(group_scores - group_max[:, None, :, :, None])
            / group_total[:, None, :, :, None]
        )
        group_dprobs = jnp.einsum(
            "cqhd,ikhd->cihqk", group_dattn, own_values, preferred_element_type=jnp.float32
        )
        group_dscores = (group_probs * (group_dprobs - group_delta[:, None, :, :, None])).astype(
            jnp.bfloat16
        )
        key_next = carry[0] + jnp.einsum(
            "cihqk,cqhd->ikhd", group_dscores, group_query, preferred_element_type=jnp.float32
        )
        value_next = carry[1] + jnp.einsum(
            "cihqk,cqhd->ikhd",
            group_probs.astype(jnp.bfloat16),
            group_dattn,
            preferred_element_type=jnp.float32,
        )
        return ((key_next, value_next), None)

    zero_sum = jnp.zeros((local_blocks, BLOCK, HEADS, HEAD_DIM), jnp.float32)
    group_inputs = (
        regroup(gathered_query),
        regroup(gathered_dattn),
        regroup(gathered_max),
        regroup(gathered_total),
        regroup(gathered_delta),
        regroup(listed),
    )
    (key_heads, value_heads), _ = lax.scan(accumulate, (zero_sum, zero_sum), group_inputs)
    key_sum = (key_heads * score_scale).reshape(local_blocks, BLOCK, -1)
    value_sum = value_heads.reshape(local_blocks, BLOCK, -1)
    d_keys = key_sum.astype(jnp.bfloat16).reshape(row_count, -1)
    d_values = value_sum.astype(jnp.bfloat16).reshape(row_count, -1)
    stacked = jnp.concatenate([d_queries, d_keys, d_values], axis=1)
    w_joined = jnp.concatenate([w_query, w_key, w_value], axis=1)
    d_inputs = lax.dot_general(
        stacked, w_joined, (((1,), (1,)), ((), ())), preferred_element_type=jnp.float32
    ).astype(jnp.bfloat16)
    grad_joined = lax.dot_general(
        inputs, stacked, (((0,), (0,)), ((), ())), preferred_element_type=jnp.float32
    )
    width_model = inputs.shape[1]
    grad_three = jnp.transpose(grad_joined.reshape(width_model, 3, -1), (1, 0, 2))
    grads = jnp.concatenate([grad_three, grad_out[None]], axis=0)
    summed = lax.psum_scatter(grads, ("seq", "rep"), scatter_dimension=1, tiled=True)
    return (output[None], d_inputs[None], summed)


def solution(mesh):
    placed = (
        P("rep", "seq", None),
        P("rep", "seq", None),
        P(),
        P("rep", None, None),
        P("rep", None),
    )
    return jax.shard_map(
        body,
        mesh=mesh,
        in_specs=placed,
        out_specs=(P("rep", "seq", None), P("rep", "seq", None), P(None, ("seq", "rep"), None)),
        check_vma=False,
    )
```

profile of v0, /device:TPU:97, one launch (start us, length us, event | category | flops | bytes accessed | tf_op | source)
XLA Modules:
  0.0 669.6 jit_solution(1449751588284421774)
XLA Ops:
  24.6 39.4 %all-gather.11.cloned.1.call-done = bf16[4096,512]{1,0:T(8,128)(2,1)} async-done(((bf16[128,512]{1,0:T(8,128)(2,1)}), bf16[4096,512]{1,0:T(8,128)(2,1)}) %all-gather.11.cloned.1.call-update) | async-done | bytes 4194320 | tf_op jit(solution)/shard_map/all_gather | solution.py:41
  63.9 4.8 gather_fusion
  68.8 48.2 %all-gather.13.cloned.1.call-done = bf16[4096,512]{1,0:T(8,128)(2,1)} async-done(((bf16[128,512]{1,0:T(8,128)(2,1)}), bf16[4096,512]{1,0:T(8,128)(2,1)}) %all-gather.13.cloned.1.call-update) | async-done | bytes 4194320 | tf_op jit(solution)/shard_map/all_gather | solution.py:40
  117.0 4.8 gather_fusion.1
  121.8 6.7 bitcast_select_fusion.1
  128.4 7.8 %copy.59 = bf16[1,27,128,512]{2,1,3,0:T(8,128)(2,1)} copy(bf16[1,27,128,512]{3,2,1,0:T(8,128)(2,1)} %get-tuple-element.173) | data formatting | bytes 7077888 | tf_op jit(solution)/shard_map/jit(_take)/select_n | solution.py:50
  136.3 7.0 %reshape.273 = bf16[3456,8,64]{0,2,1:T(8,128)(2,1)} reshape(bf16[1,27,128,512]{2,1,3,0:T(8,128)(2,1)} %copy.59) | data formatting | bytes 7077888 | tf_op jit(solution)/shard_map/reshape.48
  143.2 7.8 %copy.57 = bf16[1,27,128,512]{2,1,3,0:T(8,128)(2,1)} copy(bf16[1,27,128,512]{3,2,1,0:T(8,128)(2,1)} %get-tuple-element.174) | data formatting | bytes 7077888 | tf_op jit(solution)/shard_map/jit(_take)/select_n | solution.py:53
  151.0 7.0 %reshape.270 = bf16[3456,8,64]{0,2,1:T(8,128)(2,1)} reshape(bf16[1,27,128,512]{2,1,3,0:T(8,128)(2,1)} %copy.57) | data formatting | bytes 7077888 | tf_op jit(solution)/shard_map/reshape.51
  158.0 9.3 %fusion.27 = (f32[8,128]{1,0:T(8,128)S(1)}, f32[8,128,3456]{2,1,0:T(8,128)}) fusion(pred[3456]{0:T(1024)(128)(4,1)S(1)} %fusion.69, bf16[128,8,64]{0,2,1:T(8,128)(2,1)S(1)} %bitcast.237, bf16[3456,8,64]{0,2,1:T(8,128)(2,1)} %reshape.273), kind=kOutput, calls=%fused_computation.36 | convolution fusion | flops 463600640 | bytes 17833344 | tf_op jit(solution)/shard_map/bqhd,bkhd->bhqk/dot_general | solution.py:57
  167.2 26.0 %all-gather.3 = f32[256,128]{1,0:T(8,128)} all-gather(f32[8,128]{1,0:T(8,128)S(1)} %get-tuple-element.175), channel_id=5, replica_groups=mesh['seq'=32,'rep'=8] {'seq'}, dimensions={0}, use_global_device_ids=true | all-gather | bytes 135168 | tf_op jit(solution)/shard_map/all_gather | solution.py:108
  193.2 8.2 %fusion.28 = f32[8,128]{1,0:T(8,128)S(1)} fusion(f32[8,128,3456]{2,1,0:T(8,128)} %get-tuple-element.176, f32[8,128]{1,0:T(8,128)S(1)} %get-tuple-element.175, pred[3456]{0:T(1024)(128)(4,1)S(1)} %fusion.69), kind=kLoop, calls=%fused_computation.38 | loop fusion | flops 14154752 | bytes 14167424 | tf_op jit(solution)/shard_map/reduce_sum | solution.py:64
  201.4 25.0 %all-gather.4 = f32[256,128]{1,0:T(8,128)} all-gather(f32[8,128]{1,0:T(8,128)S(1)} %fusion.28), channel_id=6, replica_groups=mesh['seq'=32,'rep'=8] {'seq'}, dimensions={0}, use_global_device_ids=true | all-gather | bytes 135168 | tf_op jit(solution)/shard_map/all_gather | solution.py:109
  226.4 9.1 %multiply_reduce_fusion = (f32[128,8]{0,1:T(8,128)S(1)}, bf16[1,128,8,64]{1,3,2,0:T(8,128)(2,1)}) fusion(f32[1,128,8,64]{1,3,2,0:T(8,128)S(1)} %bitcast.247, f32[128,8]{0,1:T(8,128)S(1)} %bitcast.254, bf16[3456,8,64]{0,2,1:T(8,128)(2,1)S(1)} %copy-done.3, f32[8,128,3456]{2,1,0:T(8,128)} %get-tuple-element.176, f32[8,128]{1,0:T(8,128)S(1)} %get-tuple-element.175, ...), kind=kOutput, calls=%fused_computation.81 | convolution fusion | flops 467467264 | bytes 18103680 | tf_op jit(solution)/shard_map/bhqk,bkhd->bqhd/dot_general | solution.py:65
  235.5 25.4 %all_gather.27 = f32[32,8,128]{2,1,0:T(8,128)} all-gather(f32[1,8,128]{2,1,0:T(8,128)S(1)} %bitcast.255), channel_id=1, replica_groups=mesh['seq'=32,'rep'=8] {'seq'}, dimensions={0}, use_global_device_ids=true | all-gather | bytes 135168 | tf_op jit(solution)/shard_map/all_gather | solution.py:110
  260.9 88.9 %while.13 = (s32[]{:T(128)}, f32[1,128,8,64]{1,3,2,0:T(8,128)}, f32[1,128,8,64]{1,3,2,0:T(8,128)}, bf16[4,8,128,512]{3,2,1,0:T(8,128)(2,1)}, pred[4,8,1]{1,2,0:T...) while((s32[]{:T(128)}, f32[1,128,8,64]{1,3,2,0:T(8,128)}, ...), condition=%wide.region_5.7_spmd.clone, body=%wide.region_4.6_spmd.clone.sunk | while | flops 545521664 | bytes 35356956 | solution.py:165
  266.2 5.4 fusion.112
  288.4 5.4 fusion.112
  310.6 5.4 fusion.112
  332.8 5.4 fusion.112
  351.7 10.6 %fusion.51 = bf16[8,64,128]{2,1,0:T(8,128)(2,1)S(1)} fusion(bf16[3456,8,64]{0,2,1:T(8,128)(2,1)} %reshape.273, bf16[128,8,64]{0,2,1:T(8,128)(2,1)} %bitcast.252, bf16[3456,8,64]{0,2,1:T(8,128)(2,1)} %reshape.270, f32[8,128,3456]{2,1,0:T(8,128)} %get-tuple-element.176, f32[8,128]{1,0:T(8,128)S(1)} %bitcast.256, f32[8,128]{1,0:T(8,128)S(1)} %fusion.28, ...), kind=kOutput, calls=%fused_computation.62 | convolution fusion | flops 930873344 | bytes 21511552 | tf_op jit(solution)/shard_map/bhqk,bkhd->bqhd/dot_general | solution.py:97
  365.9 6.6 copy.70
  374.8 7.6 %pad_maximum_fusion = f32[4,1024,512]{2,1,0:T(8,128)} fusion(f32[1,1024,512]{2,1,0:T(8,128)} %copy.71, f32[3,1024,512]{2,1,0:T(8,128)} %bitcast.230), kind=kLoop, calls=%fused_computation.37 | loop fusion | flops 2097152 | bytes 16777216 | tf_op jit(solution)/shard_map/concatenate | solution.py:180
  388.8 272.8 %all-reduce.3.cloned.1.call-done = f32[4,1024,512]{2,1,0:T(8,128)} async-done(((f32[4,1024,512]{2,1,0:T(8,128)}), f32[4,1024,512]{2,1,0:T(8,128)}) %all-reduce.3.cloned.1.call-update) | async-done | bytes 8388624
  (137 shorter events, 99.8 us)
Async XLA Ops:
  7.2 14.7 %copy-start.11 = (s32[1,32]{1,0:T(1,128)S(1)}, s32[1,32]{1,0:T(1,128)}, u32[]{:S(2)}) copy-start(s32[1,32]{1,0:T(1,128)} %param.13) | copy-start | bytes 388
  7.2 15.3 %copy-start.10 = (s32[1,32,27]{1,0,2:T(1,128)S(1)}, s32[1,32,27]{1,0,2:T(1,128)}, u32[]{:S(2)}) copy-start(s32[1,32,27]{1,0,2:T(1,128)} %param.12) | copy-start | bytes 10372
  7.2 56.7 %all-gather.11.cloned.1.call-start = ((), (), s32[]{:S(2)}) async-start(), calls=%async_computation | async-start | bytes 4325376 | tf_op jit(solution)/shard_map/all_gather | solution.py:41
  10.3 11.4 %copy-start.4 = (bf16[128,512]{1,0:T(8,128)(2,1)S(1)}, bf16[128,512]{1,0:T(8,128)(2,1)}, u32[]{:S(2)}) copy-start(bf16[128,512]{1,0:T(8,128)(2,1)} %convolution_convert_fusion.4) | copy-start | bytes 393220
  10.3 106.7 %all-gather.13.cloned.1.call-start = ((), (), s32[]{:S(2)}) async-start(), calls=%async_computation.1 | async-start | bytes 4325376 | tf_op jit(solution)/shard_map/all_gather | solution.py:40
  12.6 8.4 %copy-start.5 = (bf16[128,512]{1,0:T(8,128)(2,1)S(1)}, bf16[128,512]{1,0:T(8,128)(2,1)}, u32[]{:S(2)}) copy-start(bf16[128,512]{1,0:T(8,128)(2,1)} %convolution_convert_fusion.2) | copy-start | bytes 393220
  12.6 248.3 %all-gather.17.cloned.1.call-start = ((), (), s32[]{:S(2)}) async-start(), calls=%async_computation.3 | async-start | bytes 4325376 | tf_op jit(solution)/shard_map/all_gather | solution.py:105
  15.0 245.9 %all-gather.15.cloned.1.call-start = ((), (), s32[]{:S(2)}) async-start(), calls=%async_computation.2 | async-start | bytes 4325376 | tf_op jit(solution)/shard_map/all_gather | solution.py:104
  17.2 644.4 %all-reduce.3.cloned.1.call-start = ((), (), s32[]{:S(2)}) async-start(), calls=%async_computation.4 | async-start | bytes 16777216
  193.2 33.2 %copy-start.3 = (bf16[3456,8,64]{0,2,1:T(8,128)(2,1)S(1)}, bf16[3456,8,64]{0,2,1:T(8,128)(2,1)}, u32[]{:S(2)}) copy-start(bf16[3456,8,64]{0,2,1:T(8,128)(2,1)} %reshape.270) | copy-start | bytes 10616836
  272.2 5.3 copy-start.7
  273.1 6.6 copy-start.1
  279.7 2.8 copy-start.8
  294.4 5.3 copy-start.7
  295.3 6.6 copy-start.1
  301.9 2.8 copy-start.8
  316.6 5.3 copy-start.7
  317.4 6.6 copy-start.1
  324.0 2.8 copy-start.8
  338.8 5.3 copy-start.7
  339.6 6.6 copy-start.1
  346.3 2.8 copy-start.8
  365.9 6.6 copy-start.6
  365.9 6.6 copy-start.9
  (5 other events, 3.8 us)
Sparse Core Ops, SparseCore 0:
  10.6 53.3 all-gather.10
  66.5 50.4 all-gather.12
  119.6 50.4 all-gather.16
  172.5 50.6 all-gather.14
  382.6 279.0 all-reduce.2
where the time goes:
time: 672 us; the launch traced here: 670 us
  waiting for transfers between devices  361 us (54%)
  matrix products  105 us (16%)
  local copies, waits for them, and re-layouts  88 us (13%)
  blocking collectives  76.3 us (11%)
  other arithmetic  25.2 us (4%)
  between operations  13.9 us (2%)
    unnamed x6, waiting for transfers between devices  273 us
    all_gather x1, waiting for transfers between devices, body(): lax.all_gather(key_rows, 'seq', axis=0, tiled=True)  48.2 us
    all_gather x1, waiting for transfers between devices, body(): lax.all_gather(value_rows, 'seq', axis=0, tiled=True)  39.4 us
    all_gather x1, blocking collectives, body(): lax.all_gather(row_max, 'seq', axis=0, tiled=True)  26 us
    all_gather x1, blocking collectives, body(): lax.all_gather(row_delta, 'seq', axis=0, tiled=True)  25.4 us
    all_gather x1, blocking collectives, body(): lax.all_gather(totals, 'seq', axis=0, tiled=True)  25 us
    dynamic_slice x32, local copies, waits for them, and re-layouts, body(): lax.scan(accumulate, (zero_sum, zero_sum), group_inputs)  24.2 us
    dot_general x4, matrix products, accumulate(): jnp.einsum('cqhd,ikhd->cihqk', group_query, own_keys, preferred_element_t...  21.5 us
  transfers between devices with their start and end apart: 5, of which 3 were waited for; matrix products, arithmetic and copies ran while one was open for 14% of the time, Pallas kernels for 0%

commit v1 on v0

--- a/solution.py
+++ b/solution.py
@@ -15,6 +15,16 @@
 
 
 def body(tokens, cotangent, weights, neighbour_lists, neighbour_counts):
+
+    def follow_matrix(inner_x, chip_axis):
+        later = lax.all_to_all(
+            jnp.stack([inner_x for _ in range(lax.axis_size(chip_axis))], axis=0),
+            axis_name=chip_axis,
+            split_axis=0,
+            concat_axis=0,
+        )
+        return jnp.concatenate(later, 0)
+
     score_scale = 1.0 / math.sqrt(HEAD_DIM)
     inputs = tokens[0]
     upstream = cotangent[0]
@@ -38,7 +48,7 @@
     )
     all_keys, all_values = (
         lax.all_gather(key_rows, "seq", axis=0, tiled=True),
-        lax.all_gather(value_rows, "seq", axis=0, tiled=True),
+        follow_matrix(value_rows, "seq"),
     )
     slab_blocks = all_keys.shape[0]
     first_block = lax.axis_index("seq") * local_blocks

time: 672 us -> 645 us (0.960)
  waiting for transfers between devices: 361 us -> 327 us
  starting transfers between devices: 0.21 us -> 8.13 us
    all_to_all x0 -> x1, waiting for transfers between devices: none -> 50.7 us  [follow_matrix(): lax.all_to_all(jnp.stack([inner_x for _ in range(lax.axis_size(chip_axis)...]
    all_gather x1, waiting for transfers between devices: 48.2 us -> 2.85 us  [body(): lax.all_gather(key_rows, 'seq', axis=0, tiled=True)]
    all_gather x1 -> x0, waiting for transfers between devices: 39.4 us -> none  [body(): lax.all_gather(value_rows, 'seq', axis=0, tiled=True)]
    all_to_all x0 -> x1, starting transfers between devices: none -> 7.96 us  [follow_matrix(): lax.all_to_all(jnp.stack([inner_x for _ in range(lax.axis_size(chip_axis)...]
    another operation x2 -> x3, local copies, waits for them, and re-layouts: 13.9 us -> 16.4 us
    unnamed x6 -> x5, waiting for transfers between devices: 273 us -> 274 us
where the time goes in v1:
time: 645 us; the launch traced here: 643 us
  waiting for transfers between devices  327 us (51%)
  matrix products  104 us (16%)
  local copies, waits for them, and re-layouts  87.8 us (14%)
  blocking collectives  75.5 us (12%)
  other arithmetic  25.2 us (4%)
  between operations  13.9 us (2%)
  starting transfers between devices  8.13 us (1%)
    unnamed x5, waiting for transfers between devices  274 us
    all_to_all x1, waiting for transfers between devices, follow_matrix(): lax.all_to_all(jnp.stack([inner_x for _ in range(lax.axis_size(chip_axis)...  50.7 us
    all_gather x1, blocking collectives, body(): lax.all_gather(totals, 'seq', axis=0, tiled=True)  26 us
    all_gather x1, blocking collectives, body(): lax.all_gather(row_max, 'seq', axis=0, tiled=True)  25.2 us
    all_gather x1, blocking collectives, body(): lax.all_gather(row_delta, 'seq', axis=0, tiled=True)  24.3 us
    dynamic_slice x32, local copies, waits for them, and re-layouts, body(): lax.scan(accumulate, (zero_sum, zero_sum), group_inputs)  24.2 us
    dot_general x4, matrix products, accumulate(): jnp.einsum('cqhd,ikhd->cihqk', group_query, own_keys, preferred_element_t...  21.5 us
    dot_general x4, matrix products, accumulate(): jnp.einsum('cqhd,ikhd->cihqk', group_dattn, own_values, preferred_element...  17.8 us
  transfers between devices with their start and end apart: 5, of which 3 were waited for; matrix products, arithmetic and copies ran while one was open for 14% of the time, Pallas kernels for 0%

profile of v1, /device:TPU:97, one launch (start us, length us, event | category | flops | bytes accessed | tf_op | source)
XLA Modules:
  0.0 642.7 jit_solution(13522044247797428555)
XLA Ops:
  19.0 8.0 %all-to-all-start = ((bf16[32,1,128,512]{3,2,1,0:T(8,128)(2,1)}), bf16[32,1,128,512]{3,2,1,0:T(8,128)(2,1)}, u32[]{:S(2)}, u32[]{:S(2)}) async-start(bf16[32,1,128,512]{3,2,1,0:T(8,128)(2,1)} %stack.3), calls=%async_computation | async-start | bytes 8388608 | tf_op jit(solution)/shard_map/all_to_all | solution.py:20
  31.6 50.7 %all-to-all-done = bf16[32,1,128,512]{3,2,1,0:T(8,128)(2,1)} async-done(((bf16[32,1,128,512]{3,2,1,0:T(8,128)(2,1)}), bf16[32,1,128,512]{3,2,1,0:T(8,128)(2,1)}, u32[]{:S(2)}, u32[]{:S(2)}) %all-to-all-start) | async-done | bytes 4194336 | tf_op jit(solution)/shard_map/all_to_all | solution.py:20
  82.3 4.9 gather_fusion
  90.1 4.8 gather_fusion.1
  94.8 6.7 %bitcast_select_fusion.1 = (bf16[1,27,128,512]{3,2,1,0:T(8,128)(2,1)}, bf16[1,27,128,512]{3,2,1,0:T(8,128)(2,1)}) fusion(bf16[27,128,512]{2,1,0:T(8,128)(2,1)} %gather_fusion.1, pred[27]{0:T(512)(128)(4,1)S(1)} %and_bitcast_fusion, bf16[27,128,512]{2,1,0:T(8,128)(2,1)} %gather_fusion), kind=kLoop, calls=%fused_computation.42 | loop fusion | flops 3538944 | bytes 14155803 | tf_op jit(solution)/shard_map/jit(_take)/select_n | solution.py:60
  101.5 7.8 %copy.59 = bf16[1,27,128,512]{2,1,3,0:T(8,128)(2,1)} copy(bf16[1,27,128,512]{3,2,1,0:T(8,128)(2,1)} %get-tuple-element.173) | data formatting | bytes 7077888 | tf_op jit(solution)/shard_map/jit(_take)/select_n | solution.py:60
  109.3 7.0 %reshape.275 = bf16[3456,8,64]{0,2,1:T(8,128)(2,1)} reshape(bf16[1,27,128,512]{2,1,3,0:T(8,128)(2,1)} %copy.59) | data formatting | bytes 7077888 | tf_op jit(solution)/shard_map/reshape.49
  116.3 7.8 %copy.57 = bf16[1,27,128,512]{2,1,3,0:T(8,128)(2,1)} copy(bf16[1,27,128,512]{3,2,1,0:T(8,128)(2,1)} %get-tuple-element.174) | data formatting | bytes 7077888 | tf_op jit(solution)/shard_map/jit(_take)/select_n | solution.py:63
  124.1 7.0 %reshape.272 = bf16[3456,8,64]{0,2,1:T(8,128)(2,1)} reshape(bf16[1,27,128,512]{2,1,3,0:T(8,128)(2,1)} %copy.57) | data formatting | bytes 7077888 | tf_op jit(solution)/shard_map/reshape.52
  131.1 9.2 %fusion.27 = (f32[8,128]{1,0:T(8,128)S(1)}, f32[8,128,3456]{2,1,0:T(8,128)}) fusion(pred[3456]{0:T(1024)(128)(4,1)S(1)} %fusion.69, bf16[128,8,64]{0,2,1:T(8,128)(2,1)S(1)} %bitcast.236, bf16[3456,8,64]{0,2,1:T(8,128)(2,1)} %reshape.275), kind=kOutput, calls=%fused_computation.36 | convolution fusion | flops 463600640 | bytes 17833344 | tf_op jit(solution)/shard_map/bqhd,bkhd->bhqk/dot_general | solution.py:67
  140.3 25.2 %all-gather.2 = f32[256,128]{1,0:T(8,128)} all-gather(f32[8,128]{1,0:T(8,128)S(1)} %get-tuple-element.175), channel_id=4, replica_groups=mesh['seq'=32,'rep'=8] {'seq'}, dimensions={0}, use_global_device_ids=true | all-gather | bytes 135168 | tf_op jit(solution)/shard_map/all_gather | solution.py:118
  165.5 8.3 %fusion.28 = f32[8,128]{1,0:T(8,128)S(1)} fusion(f32[8,128,3456]{2,1,0:T(8,128)} %get-tuple-element.176, f32[8,128]{1,0:T(8,128)S(1)} %get-tuple-element.175, pred[3456]{0:T(1024)(128)(4,1)S(1)} %fusion.69), kind=kLoop, calls=%fused_computation.38 | loop fusion | flops 14154752 | bytes 14167424 | tf_op jit(solution)/shard_map/reduce_sum | solution.py:74
  173.7 26.0 %all-gather.3 = f32[256,128]{1,0:T(8,128)} all-gather(f32[8,128]{1,0:T(8,128)S(1)} %fusion.28), channel_id=5, replica_groups=mesh['seq'=32,'rep'=8] {'seq'}, dimensions={0}, use_global_device_ids=true | all-gather | bytes 135168 | tf_op jit(solution)/shard_map/all_gather | solution.py:119
  199.7 9.1 %multiply_reduce_fusion = (f32[128,8]{0,1:T(8,128)S(1)}, bf16[1,128,8,64]{1,3,2,0:T(8,128)(2,1)}) fusion(f32[1,128,8,64]{1,3,2,0:T(8,128)S(1)} %bitcast.246, f32[128,8]{0,1:T(8,128)S(1)} %bitcast.253, bf16[3456,8,64]{0,2,1:T(8,128)(2,1)S(1)} %copy-done.3, f32[8,128,3456]{2,1,0:T(8,128)} %get-tuple-element.176, f32[8,128]{1,0:T(8,128)S(1)} %get-tuple-element.175, ...), kind=kOutput, calls=%fused_computation.81 | convolution fusion | flops 467467264 | bytes 18103680 | tf_op jit(solution)/shard_map/bhqk,bkhd->bqhd/dot_general | solution.py:75
  208.8 24.3 %all_gather.23 = f32[32,8,128]{2,1,0:T(8,128)} all-gather(f32[1,8,128]{2,1,0:T(8,128)S(1)} %bitcast.254), channel_id=1, replica_groups=mesh['seq'=32,'rep'=8] {'seq'}, dimensions={0}, use_global_device_ids=true | all-gather | bytes 135168 | tf_op jit(solution)/shard_map/all_gather | solution.py:120
  233.1 88.9 %while.13 = (s32[]{:T(128)}, f32[1,128,8,64]{1,3,2,0:T(8,128)}, f32[1,128,8,64]{1,3,2,0:T(8,128)}, bf16[4,8,128,512]{3,2,1,0:T(8,128)(2,1)}, pred[4,8,1]{1,2,0:T...) while((s32[]{:T(128)}, f32[1,128,8,64]{1,3,2,0:T(8,128)}, ...), condition=%wide.region_5.7_spmd.clone, body=%wide.region_4.6_spmd.clone.sunk | while | flops 545521664 | bytes 35356956 | solution.py:175
  238.4 5.4 fusion.112
  260.6 5.4 fusion.112
  282.8 5.4 fusion.112
  305.0 5.4 fusion.112
  323.9 10.6 %fusion.51 = bf16[8,64,128]{2,1,0:T(8,128)(2,1)S(1)} fusion(bf16[3456,8,64]{0,2,1:T(8,128)(2,1)} %reshape.275, bf16[128,8,64]{0,2,1:T(8,128)(2,1)} %bitcast.251, bf16[3456,8,64]{0,2,1:T(8,128)(2,1)} %reshape.272, f32[8,128,3456]{2,1,0:T(8,128)} %get-tuple-element.176, f32[8,128]{1,0:T(8,128)S(1)} %bitcast.255, f32[8,128]{1,0:T(8,128)S(1)} %fusion.28, ...), kind=kOutput, calls=%fused_computation.62 | convolution fusion | flops 930873344 | bytes 21511552 | tf_op jit(solution)/shard_map/bhqk,bkhd->bqhd/dot_general | solution.py:107
  338.1 6.6 %copy.70 = f32[1024,3,512]{2,0,1:T(8,128)} copy(f32[1024,3,512]{0,2,1:T(8,128)} %bitcast.227) | data formatting | bytes 12582912 | tf_op jit(solution)/shard_map/reshape | solution.py:189
  347.0 7.6 %pad_maximum_fusion = f32[4,1024,512]{2,1,0:T(8,128)} fusion(f32[1,1024,512]{2,1,0:T(8,128)} %copy.71, f32[3,1024,512]{2,1,0:T(8,128)} %bitcast.230), kind=kLoop, calls=%fused_computation.37 | loop fusion | flops 2097152 | bytes 16777216 | tf_op jit(solution)/shard_map/concatenate | solution.py:190
  361.0 273.6 %all-reduce.3.cloned.1.call-done = f32[4,1024,512]{2,1,0:T(8,128)} async-done(((f32[4,1024,512]{2,1,0:T(8,128)}), f32[4,1024,512]{2,1,0:T(8,128)}) %all-reduce.3.cloned.1.call-update) | async-done | bytes 8388624
  (139 shorter events, 101.7 us)
Async XLA Ops:
  7.2 82.9 %all-gather.9.cloned.1.call-start = ((), (), s32[]{:S(2)}) async-start(), calls=%async_computation.1 | async-start | bytes 4325376 | tf_op jit(solution)/shard_map/all_gather | solution.py:50
  10.3 222.8 %all-gather.13.cloned.1.call-start = ((), (), s32[]{:S(2)}) async-start(), calls=%async_computation.3 | async-start | bytes 4325376 | tf_op jit(solution)/shard_map/all_gather | solution.py:115
  12.7 220.4 %all-gather.11.cloned.1.call-start = ((), (), s32[]{:S(2)}) async-start(), calls=%async_computation.2 | async-start | bytes 4325376 | tf_op jit(solution)/shard_map/all_gather | solution.py:114
  19.0 8.0 %copy-start.5 = (bf16[128,512]{1,0:T(8,128)(2,1)S(1)}, bf16[128,512]{1,0:T(8,128)(2,1)}, u32[]{:S(2)}) copy-start(bf16[128,512]{1,0:T(8,128)(2,1)} %convolution_convert_fusion.3) | copy-start | bytes 393220
  19.0 8.2 %copy-start.4 = (bf16[128,512]{1,0:T(8,128)(2,1)S(1)}, bf16[128,512]{1,0:T(8,128)(2,1)}, u32[]{:S(2)}) copy-start(bf16[128,512]{1,0:T(8,128)(2,1)} %convolution_convert_fusion.1) | copy-start | bytes 393220
  19.0 9.1 %copy-start.6 = (bf16[128,512]{1,0:T(8,128)(2,1)S(1)}, bf16[128,512]{1,0:T(8,128)(2,1)}, u32[]{:S(2)}) copy-start(bf16[128,512]{1,0:T(8,128)(2,1)} %convolution_convert_fusion.2) | copy-start | bytes 393220
  19.0 10.0 %copy-start.12 = (s32[1,32]{1,0:T(1,128)S(1)}, s32[1,32]{1,0:T(1,128)}, u32[]{:S(2)}) copy-start(s32[1,32]{1,0:T(1,128)} %param.13) | copy-start | bytes 388
  19.0 10.5 %copy-start.11 = (s32[1,32,27]{1,0,2:T(1,128)S(1)}, s32[1,32,27]{1,0,2:T(1,128)}, u32[]{:S(2)}) copy-start(s32[1,32,27]{1,0,2:T(1,128)} %param.12) | copy-start | bytes 10372
  19.0 63.3 %all-to-all-start = ((bf16[32,1,128,512]{3,2,1,0:T(8,128)(2,1)}), bf16[32,1,128,512]{3,2,1,0:T(8,128)(2,1)}, u32[]{:S(2)}, u32[]{:S(2)}) async-start(bf16[32,1,128,512]{3,2,1,0:T(8,128)(2,1)} %stack.3), calls=%async_computation | async-start | bytes 8388608 | tf_op jit(solution)/shard_map/all_to_all | solution.py:20
  26.9 607.7 %all-reduce.3.cloned.1.call-start = ((), (), s32[]{:S(2)}) async-start(), calls=%async_computation.4 | async-start | bytes 16777216
  165.4 34.3 %copy-start.3 = (bf16[3456,8,64]{0,2,1:T(8,128)(2,1)S(1)}, bf16[3456,8,64]{0,2,1:T(8,128)(2,1)}, u32[]{:S(2)}) copy-start(bf16[3456,8,64]{0,2,1:T(8,128)(2,1)} %reshape.272) | copy-start | bytes 10616836
  244.5 5.3 copy-start.8
  245.3 6.6 %copy-start.1 = (f32[1,128,8,64]{1,3,2,0:T(8,128)S(1)}, f32[1,128,8,64]{1,3,2,0:T(8,128)}, u32[]{:S(2)}) copy-start(f32[1,128,8,64]{1,3,2,0:T(8,128)} %get-tuple-element.269) | copy-start | bytes 786436 | tf_op jit(solution)/shard_map/while
  251.9 2.8 copy-start.9
  266.7 5.3 copy-start.8
  267.5 6.6 %copy-start.1 = (f32[1,128,8,64]{1,3,2,0:T(8,128)S(1)}, f32[1,128,8,64]{1,3,2,0:T(8,128)}, u32[]{:S(2)}) copy-start(f32[1,128,8,64]{1,3,2,0:T(8,128)} %get-tuple-element.269) | copy-start | bytes 786436 | tf_op jit(solution)/shard_map/while
  274.1 2.8 copy-start.9
  288.8 5.3 copy-start.8
  289.6 6.6 %copy-start.1 = (f32[1,128,8,64]{1,3,2,0:T(8,128)S(1)}, f32[1,128,8,64]{1,3,2,0:T(8,128)}, u32[]{:S(2)}) copy-start(f32[1,128,8,64]{1,3,2,0:T(8,128)} %get-tuple-element.269) | copy-start | bytes 786436 | tf_op jit(solution)/shard_map/while
  296.3 2.8 copy-start.9
  311.1 5.3 copy-start.8
  311.9 6.6 %copy-start.1 = (f32[1,128,8,64]{1,3,2,0:T(8,128)S(1)}, f32[1,128,8,64]{1,3,2,0:T(8,128)}, u32[]{:S(2)}) copy-start(f32[1,128,8,64]{1,3,2,0:T(8,128)} %get-tuple-element.269) | copy-start | bytes 786436 | tf_op jit(solution)/shard_map/while
  338.1 6.6 %copy-start.7 = (bf16[1,128,1024]{2,1,0:T(8,128)(2,1)S(1)}, bf16[1,128,1024]{2,1,0:T(8,128)(2,1)}, u32[]{:S(2)}) copy-start(bf16[1,128,1024]{2,1,0:T(8,128)(2,1)} %param.10) | copy-start | bytes 786436
  338.1 6.6 %copy-start.10 = (bf16[1,128,8,64]{1,3,2,0:T(8,128)(2,1)S(1)}, bf16[1,128,8,64]{1,3,2,0:T(8,128)(2,1)}, u32[]{:S(2)}) copy-start(bf16[1,128,8,64]{1,3,2,0:T(8,128)(2,1)} %get-tuple-element.178) | copy-start | bytes 393220
  (6 other events, 6.6 us)
Sparse Core Ops, SparseCore 0:
  10.5 79.4 all-gather.8
  92.6 50.7 all-gather.12
  146.0 50.8 all-gather.10
  354.8 279.8 all-reduce.2
